TPU v7x, 256 devices: a whole 4x4x8 slice. The times are simulated.
256 devices in a mesh: coarse: 8 (over x, core), fine: 32 (over z, y).
Axes of the slice: x: 4, y: 4, z: 8, core: 2. Of those that a mesh axis runs over, the one named last changes fastest.
Arguments:
- tokens: bfloat16 [131072, 1024], P(('coarse', 'fine'))
- w_qkv: bfloat16 [1024, 3072], replicated, may hold values from -0.1875 to 0.1875
- w_coarse_out: bfloat16 [1024, 1024], replicated, may hold values from -0.1875 to 0.1875
- w_kv2: bfloat16 [1024, 2048], replicated, may hold values from -0.1875 to 0.1875
- w_out: bfloat16 [1024, 1024], replicated, may hold values from -0.1875 to 0.1875
- seg_start: int32 [4096], P('coarse'), may hold values from 0 to 131071, as said below
- seg_end: int32 [4096], P('coarse'), may hold values from 1 to 131072, as said below
- block_lists: int32 [512, 8], P(('coarse', 'fine')), may hold values from 0 to 255, as said below
Outputs:
- mixed: bfloat16 [131072, 1024], P(('coarse', 'fine'))
Inputs may be any that keep to these rules, and one draw needn't show every extreme that they name: `seg_start`: for each coarse owner c, the segments c*512 to (c+1)*512 - 1 are nonempty and pairwise disjoint and lie within time steps c*16384 to (c+1)*16384 - 1, listed in an order that does not follow time; steps outside all segments belong to none; segment lengths are uneven. seg_end[s] > seg_start[s]. `block_lists`: row n names 8 distinct coarse key blocks (block b holds segments b*16 to (b+1)*16 - 1), all among the blocks of owners c-1, c and c+1 taken cyclically over the owners, where c = n*256 // 16384 is the owner of the row's time steps.
All inputs are finite; a program needn't handle non-finite values.
Results may differ from a plain program's by a relative error of at most 0.017.
Values may be sent and summed in bfloat16 or wider, within the bound.
A program may use at most 128 MiB of HBM per device.

v0:
```python
import math
import jax
import jax.numpy as jnp
from jax import lax
from jax.sharding import PartitionSpec as P

HEADS = 8
KB = 16
QB = 256


def padded(cells, sides, width):
    for axis, dim in sides:
        count = lax.axis_size(axis)
        head = lax.slice_in_dim(cells, 0, width, axis=dim)
        tail = lax.slice_in_dim(cells, cells.shape[dim] - width, cells.shape[dim], axis=dim)
        cells = jnp.concatenate(
            [
                lax.ppermute(tail, axis, [(i, (i + 1) % count) for i in range(count)]),
                cells,
                lax.ppermute(head, axis, [((i + 1) % count, i) for i in range(count)]),
            ],
            axis=dim,
        )
    return cells


def attend_heads(queries, keys, content_elements, allowed):
    count = queries.shape[0]
    head_size = queries.shape[1] // HEADS
    query_heads = queries.reshape(count, HEADS, head_size)
    key_heads = keys.reshape(keys.shape[0], HEADS, head_size)
    value_heads = content_elements.reshape(content_elements.shape[0], HEADS, head_size)
    scores = jnp.einsum("qhd,khd->hqk", query_heads, key_heads, preferred_element_type=jnp.float32)
    scores = scores * (1.0 / math.sqrt(head_size))
    scores = jnp.where(allowed[None], scores, -1e30)
    highest = jnp.max(scores, axis=-1, keepdims=True)
    expos = jnp.exp(scores - highest)
    weights = (expos / jnp.sum(expos, axis=-1, keepdims=True)).astype(jnp.bfloat16)
    blended = jnp.einsum("hqk,khd->qhd", weights, value_heads, preferred_element_type=jnp.float32)
    return blended.astype(jnp.bfloat16).reshape(count, HEADS * head_size)


def normalize(content_elements):
    return content_elements * lax.rsqrt(
        jnp.mean(content_elements * content_elements, axis=-1, keepdims=True) + 1e-06
    )


def body(tokens, w_qkv, w_coarse_out, w_kv2, w_out, seg_start, seg_end, block_lists):
    rows_here = tokens.shape[0]
    width = tokens.shape[1]
    fine_count = lax.axis_size("fine")
    coarse_count = lax.axis_size("coarse")
    fine_index = lax.axis_index("fine")
    coarse_index = lax.axis_index("coarse")
    seg_owned = seg_start.shape[0]
    first_row = coarse_index * (rows_here * fine_count) + fine_index * rows_here
    positions = first_row + jnp.arange(rows_here, dtype=jnp.int32)
    member = (
        (positions[None, :] >= seg_start[:, None]) & (positions[None, :] < seg_end[:, None])
    ).astype(jnp.bfloat16)
    sums = lax.psum_scatter(
        jnp.dot(member, tokens, preferred_element_type=jnp.float32).astype(jnp.bfloat16),
        "fine",
        scatter_dimension=0,
        tiled=True,
    ).astype(jnp.float32)
    share_start = fine_index * KB
    spans = (
        lax.dynamic_slice_in_dim(seg_end, share_start, KB, 0)
        - lax.dynamic_slice_in_dim(seg_start, share_start, KB, 0)
    ).astype(jnp.float32)
    pooled = (sums / jnp.sqrt(spans)[:, None]).astype(jnp.bfloat16)
    coarse_proj = jnp.dot(pooled, w_qkv, preferred_element_type=jnp.float32)
    coarse_query = coarse_proj[:, :width].astype(jnp.bfloat16)
    coarse_pair = coarse_proj[:, width:].astype(jnp.bfloat16)
    owner_pairs = lax.all_gather(coarse_pair, "fine", axis=0, tiled=True)
    reach = seg_owned // 2
    window_table = padded(owner_pairs, (("coarse", 0),), reach)
    query_place = reach + share_start + jnp.arange(KB, dtype=jnp.int32)
    key_place = jnp.arange(window_table.shape[0], dtype=jnp.int32)
    allowed = jnp.abs(query_place[:, None] - key_place[None, :]) <= reach
    coarse_mix = attend_heads(
        coarse_query, window_table[:, :width], window_table[:, width:], allowed
    )
    context = jnp.dot(coarse_mix, w_coarse_out, preferred_element_type=jnp.float32)
    state = normalize(context).astype(jnp.bfloat16)
    payload = jnp.dot(state, w_kv2, preferred_element_type=jnp.float32).astype(jnp.bfloat16)
    seg_total = seg_owned * coarse_count
    owner_rows = lax.all_gather(payload, "fine", axis=0, tiled=True)
    second_table = padded(owner_rows, (("coarse", 0),), seg_owned)
    table_base = (coarse_index - 1) * seg_owned
    proj = jnp.dot(tokens, w_qkv, preferred_element_type=jnp.float32)
    query = proj[:, :width].astype(jnp.bfloat16)
    key_rows = proj[:, width : 2 * width].astype(jnp.bfloat16)
    value_rows = proj[:, 2 * width :].astype(jnp.bfloat16)
    listed_rows = (
        block_lists[:, :, None] * KB + jnp.arange(KB, dtype=jnp.int32)[None, None, :]
    ).reshape(block_lists.shape[0], -1)
    table_rows = jnp.mod(listed_rows - table_base, seg_total)
    block_rows = min(512, rows_here)
    sub_blocks = block_rows // QB
    remote_per_sub = table_rows.shape[1]
    query_group = jnp.arange(block_rows, dtype=jnp.int32) // QB
    remote_group = jnp.arange(sub_blocks * remote_per_sub, dtype=jnp.int32) // remote_per_sub
    allowed_fine = jnp.concatenate(
        [
            jnp.ones((block_rows, rows_here), dtype=bool),
            query_group[:, None] == remote_group[None, :],
        ],
        axis=1,
    )

    def query_block(number):
        wanted = table_rows.reshape(-1)
        remote = jnp.take(second_table, wanted, axis=0)
        keys = jnp.concatenate([key_rows, remote[:, :width]], axis=0)
        content_elements = jnp.concatenate([value_rows, remote[:, width:]], axis=0)
        return attend_heads(query, keys, content_elements, allowed_fine)

    attended = lax.map(query_block, jnp.arange(rows_here // block_rows, dtype=jnp.int32)).reshape(
        rows_here, width
    )
    projected = jnp.dot(attended, w_out, preferred_element_type=jnp.float32)
    return normalize(projected).astype(jnp.bfloat16)


def solution(mesh):
    placed = (
        P(("coarse", "fine"), None),
        P(),
        P(),
        P(),
        P(),
        P("coarse"),
        P("coarse"),
        P(("coarse", "fine"), None),
    )
    return jax.shard_map(
        body, mesh=mesh, in_specs=placed, out_specs=P(("coarse", "fine"), None), check_vma=False
    )
```

profile of v0, /device:TPU:1, one launch (start us, length us, event | category | flops | bytes accessed | tf_op | source)
XLA Modules:
  0.0 506.6 jit_solution(6676271423048525589)
XLA Ops:
  6.5 3.1 convolution_convert_fusion.3
  10.5 215.7 %reduce-scatter.2.cloned.1.call-done = bf16[16,1024]{1,0:T(8,128)(2,1)} async-done(((bf16[512,1024]{1,0:T(8,128)(2,1)}), bf16[16,1024]{1,0:T(8,128)(2,1)}) %reduce-scatter.2.cloned.1.call-update) | async-done | bytes 32784 | tf_op jit(solution)/shard_map/reduce_scatter | solution.py:63
  226.3 3.8 convolution_convert_fusion.1
  230.7 77.0 %all-gather.3.cloned.1.call-done = bf16[512,2048]{1,0:T(8,128)(2,1)} async-done(((bf16[16,2048]{1,0:T(8,128)(2,1)}), bf16[512,2048]{1,0:T(8,128)(2,1)}) %all-gather.3.cloned.1.call-update) | async-done | bytes 2097168 | tf_op jit(solution)/shard_map/all_gather | solution.py:78
  307.7 3.1 fusion.55
  310.8 6.5 %collective-permute-start = (bf16[256,2048]{1,0:T(8,128)(2,1)}, bf16[256,2048]{1,0:T(8,128)(2,1)}, u32[]{:S(2)}, u32[]{:S(2)}) collective-permute-start(bf16[256,2048]{1,0:T(8,128)(2,1)} %get-tuple-element.34), channel_id=1, source_target_pairs={{0,32},{32,64},{64,96},{96,128},{128,160},{160,192},{192,224},{224... | collective-permute-start | bytes 3145736 | tf_op jit(solution)/shard_map/ppermute | solution.py:19
  317.5 12.0 %collective-permute-done = bf16[256,2048]{1,0:T(8,128)(2,1)} collective-permute-done((bf16[256,2048]{1,0:T(8,128)(2,1)}, bf16[256,2048]{1,0:T(8,128)(2,1)}, u32[]{:S(2)}, u32[]{:S(2)}) %collective-permute-start) | collective-permute-done | bytes 1048608 | tf_op jit(solution)/shard_map/ppermute | solution.py:19
  331.9 2.9 slice_bitcast_fusion.1
  334.8 2.4 fusion.57
  337.2 2.4 fusion.28
  339.6 2.1 multiply_reduce_fusion.1
  341.7 1.3 convolution_convert_fusion.2
  343.4 70.0 %all-gather.5.cloned.1.call-done = bf16[512,2048]{1,0:T(8,128)(2,1)} async-done(((bf16[16,2048]{1,0:T(8,128)(2,1)}), bf16[512,2048]{1,0:T(8,128)(2,1)}) %all-gather.5.cloned.1.call-update) | async-done | bytes 2097168 | tf_op jit(solution)/shard_map/all_gather | solution.py:91
  413.4 5.5 %collective-permute-start.3 = (bf16[512,2048]{1,0:T(8,128)(2,1)}, bf16[512,2048]{1,0:T(8,128)(2,1)S(1)}, u32[]{:S(2)}, u32[]{:S(2)}) collective-permute-start(bf16[512,2048]{1,0:T(8,128)(2,1)} %all-gather.5.cloned.1.call-done), channel_id=1, source_target_pairs={{32,0},{64,32},{96,64},{128,96},{160,128},{192,160},{224,192},{0,2... | collective-permute-start | bytes 6291464 | tf_op jit(solution)/shard_map/ppermute | solution.py:21
  420.3 6.5 %convolution_convert_fusion = bf16[512,3072]{1,0:T(8,128)(2,1)S(1)} fusion(bf16[512,1024]{1,0:T(8,128)(2,1)} %param.8, bf16[1024,3072]{1,0:T(8,128)(2,1)} %param.9), kind=kOutput, calls=%fused_computation.12 | convolution fusion | flops 3222798336 | bytes 10485760 | tf_op jit(solution)/shard_map/dot_general | solution.py:94
  426.9 1.8 slice_bitcast_fusion.2
  428.6 15.6 %collective-permute-done.3 = bf16[512,2048]{1,0:T(8,128)(2,1)S(1)} collective-permute-done((bf16[512,2048]{1,0:T(8,128)(2,1)}, bf16[512,2048]{1,0:T(8,128)(2,1)S(1)}, u32[]{:S(2)}, u32[]{:S(2)}) %collective-permute-start.3) | collective-permute-done | bytes 2097184 | tf_op jit(solution)/shard_map/ppermute | solution.py:21
  444.2 11.2 %pad_maximum_fusion = bf16[1536,2048]{1,0:T(8,128)(2,1)} fusion(bf16[512,2048]{1,0:T(8,128)(2,1)S(1)} %collective-permute-done.3, bf16[512,2048]{1,0:T(8,128)(2,1)S(1)} %copy-done.5, bf16[512,2048]{1,0:T(8,128)(2,1)S(1)} %collective-permute-done.2), kind=kLoop, calls=%fused_computation.7 | loop fusion | flops 18874368 | bytes 12582912 | tf_op jit(solution)/shard_map/concatenate | solution.py:17
  455.4 6.0 %gather_fusion = bf16[256,2048]{1,0:T(8,128)(2,1)S(1)} fusion(bf16[1536,2048]{1,0:T(8,128)(2,1)} %pad_maximum_fusion, s32[1024]{0:T(1024)S(1)} %pad_clamp_fusion), kind=kCustom, calls=%fused_computation | custom fusion | bytes 2098176 | tf_op jit(solution)/shard_map/while/body/eval_jaxpr/jit(_take)/gather | solution.py:117
  464.0 2.6 copy.22
  466.6 7.7 %fusion.13 = f32[8,512,768]{2,1,0:T(8,128)} fusion(bf16[64,8,8,128]{3,2,1,0:T(8,128)(2,1)S(1)} %copy-done.4, bf16[256,1024]{1,0:T(8,128)(2,1)} %get-tuple-element.36, bf16[512,1024]{1,0:T(8,128)(2,1)} %get-tuple-element.22), kind=kOutput, calls=%fused_computation.25 | convolution fusion | flops 808452096 | bytes 15204352 | tf_op jit(solution)/shard_map/while/body/eval_jaxpr/qhd,khd->hqk/dot_general | solution.py:34
  474.3 16.3 %fusion.58 = (f32[8,512]{1,0:T(8,128)S(1)}, f32[8,512,768]{2,1,0:T(8,128)}) fusion(f32[8,512,768]{2,1,0:T(8,128)} %fusion.13, pred[512,768]{1,0:T(8,128)(4,1)S(1)} %concatenate.20), kind=kOutput, calls=%fused_computation.102 | output fusion | flops 18875136 | bytes 25575424 | tf_op jit(solution)/shard_map/while/body/eval_jaxpr/sub | solution.py:38
  490.7 6.9 %fusion.16 = bf16[8,128,512]{2,1,0:T(8,128)(2,1)S(1)} fusion(bf16[768,8,128]{0,2,1:T(8,128)(2,1)S(1)} %bitcast.73, f32[8,512,768]{2,1,0:T(8,128)} %get-tuple-element.43, f32[8,512]{1,0:T(8,128)S(1)} %get-tuple-element.42), kind=kOutput, calls=%fused_computation.31 | convolution fusion | flops 812122112 | bytes 15220736 | tf_op jit(solution)/shard_map/while/body/eval_jaxpr/hqk,khd->qhd/dot_general | solution.py:40
  497.5 1.4 multiply_reduce_fusion
  (54 shorter events, 9.6 us)
Async XLA Ops:
  6.5 491.0 %copy-start = (bf16[1024,1024]{1,0:T(8,128)(2,1)S(1)}, bf16[1024,1024]{1,0:T(8,128)(2,1)}, u32[]{:S(2)}) copy-start(bf16[1024,1024]{1,0:T(8,128)(2,1)} %param.12) | copy-start | bytes 6291460
  6.5 219.7 %reduce-scatter.2.cloned.1.call-start = ((), (), s32[]{:S(2)}) async-start(), calls=%async_computation.1 | async-start | bytes 1081344 | tf_op jit(solution)/shard_map/reduce_scatter | solution.py:63
  9.7 298.0 %all-gather.3.cloned.1.call-start = ((), (), s32[]{:S(2)}) async-start(), calls=%async_computation.2 | async-start | bytes 2162688 | tf_op jit(solution)/shard_map/all_gather | solution.py:78
  230.7 182.8 %all-gather.5.cloned.1.call-start = ((), (), s32[]{:S(2)}) async-start(), calls=%async_computation.3 | async-start | bytes 2162688 | tf_op jit(solution)/shard_map/all_gather | solution.py:91
  310.8 18.6 %collective-permute-start = (bf16[256,2048]{1,0:T(8,128)(2,1)}, bf16[256,2048]{1,0:T(8,128)(2,1)}, u32[]{:S(2)}, u32[]{:S(2)}) collective-permute-start(bf16[256,2048]{1,0:T(8,128)(2,1)} %get-tuple-element.34), channel_id=1, source_target_pairs={{0,32},{32,64},{64,96},{96,128},{128,160},{160,192},{192,224},{224... | collective-permute-start | bytes 3145736 | tf_op jit(solution)/shard_map/ppermute | solution.py:19
  317.4 14.4 %collective-permute-start.1 = (bf16[256,2048]{1,0:T(8,128)(2,1)}, bf16[256,2048]{1,0:T(8,128)(2,1)S(1)}, u32[]{:S(2)}, u32[]{:S(2)}) collective-permute-start(bf16[256,2048]{1,0:T(8,128)(2,1)} %get-tuple-element.32), channel_id=1, source_target_pairs={{32,0},{64,32},{96,64},{128,96},{160,128},{192,160},{224,192},{0,2... | collective-permute-start | bytes 3145736 | tf_op jit(solution)/shard_map/ppermute | solution.py:21
  317.4 13.4 %copy-start.1 = (bf16[512,2048]{1,0:T(8,128)(2,1)S(1)}, bf16[512,2048]{1,0:T(8,128)(2,1)}, u32[]{:S(2)}) copy-start(bf16[512,2048]{1,0:T(8,128)(2,1)} %all-gather.3.cloned.1.call-done) | copy-start | bytes 6291460
  337.2 4.5 copy-start.2
  339.6 3.5 copy-start.7
  413.4 30.8 %collective-permute-start.3 = (bf16[512,2048]{1,0:T(8,128)(2,1)}, bf16[512,2048]{1,0:T(8,128)(2,1)S(1)}, u32[]{:S(2)}, u32[]{:S(2)}) collective-permute-start(bf16[512,2048]{1,0:T(8,128)(2,1)} %all-gather.5.cloned.1.call-done), channel_id=1, source_target_pairs={{32,0},{64,32},{96,64},{128,96},{160,128},{192,160},{224,192},{0,2... | collective-permute-start | bytes 6291464 | tf_op jit(solution)/shard_map/ppermute | solution.py:21
  418.9 25.3 %collective-permute-start.2 = (bf16[512,2048]{1,0:T(8,128)(2,1)}, bf16[512,2048]{1,0:T(8,128)(2,1)S(1)}, u32[]{:S(2)}, u32[]{:S(2)}) collective-permute-start(bf16[512,2048]{1,0:T(8,128)(2,1)} %all-gather.5.cloned.1.call-done), channel_id=1, source_target_pairs={{0,32},{32,64},{64,96},{96,128},{128,160},{160,192},{192,224},{224... | collective-permute-start | bytes 6291464 | tf_op jit(solution)/shard_map/ppermute | solution.py:19
  426.9 17.3 %copy-start.5 = (bf16[512,2048]{1,0:T(8,128)(2,1)S(1)}, bf16[512,2048]{1,0:T(8,128)(2,1)}, u32[]{:S(2)}) copy-start(bf16[512,2048]{1,0:T(8,128)(2,1)} %all-gather.5.cloned.1.call-done) | copy-start | bytes 6291460
  461.4 1.3 copy-start.3
  462.7 3.9 copy-start.4
  474.3 16.3 %copy-start.6 = (bf16[768,1024]{0,1:T(8,128)(2,1)S(1)}, bf16[768,1024]{0,1:T(8,128)(2,1)}, u32[]{:S(2)}) copy-start(bf16[768,1024]{0,1:T(8,128)(2,1)} %copy.22) | copy-start | bytes 4718596
Sparse Core Ops, SparseCore 0:
  11.1 215.0 reduce-scatter.1
  230.8 76.8 all-gather.2
  343.2 70.2 all-gather.4
where the time goes:
time: 507 us
  waiting for transfers between devices  391 us (77%)
  matrix products  37.7 us (7%)
  other arithmetic  31.2 us (6%)
  local copies, waits for them, and re-layouts  20.1 us (4%)
  between operations  13.3 us (3%)
  starting transfers between devices  13.2 us (3%)
    reduce_scatter x1, waiting for transfers between devices, body(): lax.psum_scatter(jnp.dot(member, tokens, preferred_element_type=jnp.float...  216 us
    all_gather x1, waiting for transfers between devices, body(): owner_pairs = lax.all_gather(coarse_pair, 'fine', axis=0, tiled=True)  77 us
    all_gather x1, waiting for transfers between devices, body(): owner_rows = lax.all_gather(payload, 'fine', axis=0, tiled=True)  70 us
    ppermute x2, waiting for transfers between devices, padded(): lax.ppermute(head, axis, [((i + 1) % count, i) for i in range(count)])  16.5 us
    sub x1, other arithmetic, attend_heads(): expos = jnp.exp(scores - highest)  16.3 us
    ppermute x2, waiting for transfers between devices, padded(): lax.ppermute(tail, axis, [(i, (i + 1) % count) for i in range(count)])  12 us
    concatenate x1, other arithmetic, padded(): jnp.concatenate([lax.ppermute(tail, axis, [(i, (i + 1) % count) for i in...  11.2 us
  transfers between devices with their start and end apart: 7, of which 6 were waited for; matrix products, arithmetic and copies ran while one was open for 2% of the time, Pallas kernels for 0%

commit v1 on v0

--- a/solution.py
+++ b/solution.py
@@ -7,6 +7,10 @@
 HEADS = 8
 KB = 16
 QB = 256
+sites_begin = lambda page, chip_axis: jnp.concatenate(
+    lax.all_to_all(jnp.stack([page for _ in range(lax.axis_size(chip_axis))]), chip_axis, 0, 0),
+    axis=0,
+)
 
 
 def padded(cells, sides, width):
@@ -88,7 +92,7 @@
     state = normalize(context).astype(jnp.bfloat16)
     payload = jnp.dot(state, w_kv2, preferred_element_type=jnp.float32).astype(jnp.bfloat16)
     seg_total = seg_owned * coarse_count
-    owner_rows = lax.all_gather(payload, "fine", axis=0, tiled=True)
+    owner_rows = sites_begin(payload, "fine")
     second_table = padded(owner_rows, (("coarse", 0),), seg_owned)
     table_base = (coarse_index - 1) * seg_owned
     proj = jnp.dot(tokens, w_qkv, preferred_element_type=jnp.float32)

time: 507 us -> 485 us (0.957)
  waiting for transfers between devices: 391 us -> 368 us
  other arithmetic: 31.2 us -> 24.9 us
    all_gather x1 -> x0, waiting for transfers between devices: 70 us -> none  [body(): owner_rows = lax.all_gather(payload, 'fine', axis=0, tiled=True)]
    all_to_all x0 -> x1, waiting for transfers between devices: none -> 46.5 us  [lax.all_to_all(jnp.stack([page for _ in range(lax.axis_size(chip_axis))])...]
    concatenate x1, other arithmetic: 11.2 us -> 4.93 us  [padded(): jnp.concatenate([lax.ppermute(tail, axis, [(i, (i + 1) % count) for i in...]
    all_to_all x0 -> x1, starting transfers between devices: none -> 5.62 us  [lax.all_to_all(jnp.stack([page for _ in range(lax.axis_size(chip_axis))])...]
where the time goes in v1:
time: 485 us; the launch traced here: 482 us
  waiting for transfers between devices  368 us (76%)
  matrix products  37 us (8%)
  other arithmetic  24.9 us (5%)
  local copies, waits for them, and re-layouts  21.8 us (4%)
  starting transfers between devices  17.3 us (4%)
  between operations  13.6 us (3%)
    reduce_scatter x1, waiting for transfers between devices, body(): lax.psum_scatter(jnp.dot(member, tokens, preferred_element_type=jnp.float...  216 us
    all_gather x1, waiting for transfers between devices, body(): owner_pairs = lax.all_gather(coarse_pair, 'fine', axis=0, tiled=True)  77 us
    all_to_all x1, waiting for transfers between devices, lax.all_to_all(jnp.stack([page for _ in range(lax.axis_size(chip_axis))])...  46.5 us
    ppermute x2, waiting for transfers between devices, padded(): lax.ppermute(head, axis, [((i + 1) % count, i) for i in range(count)])  16.4 us
    sub x1, other arithmetic, attend_heads(): expos = jnp.exp(scores - highest)  16.2 us
    ppermute x2, waiting for transfers between devices, padded(): lax.ppermute(tail, axis, [(i, (i + 1) % count) for i in range(count)])  12 us
  transfers between devices with their start and end apart: 7, of which 6 were waited for; matrix products, arithmetic and copies ran while one was open for 2% of the time, Pallas kernels for 0%

profile of v1, /device:TPU:1, one launch (start us, length us, event | category | flops | bytes accessed | tf_op | source)
XLA Modules:
  0.0 482.3 jit_solution(3217756528330818270)
XLA Ops:
  6.5 3.1 convolution_convert_fusion.3
  10.5 215.7 %reduce-scatter.2.cloned.1.call-done = bf16[16,1024]{1,0:T(8,128)(2,1)} async-done(((bf16[512,1024]{1,0:T(8,128)(2,1)}), bf16[16,1024]{1,0:T(8,128)(2,1)}) %reduce-scatter.2.cloned.1.call-update) | async-done | bytes 32784 | tf_op jit(solution)/shard_map/reduce_scatter | solution.py:67
  226.3 3.8 convolution_convert_fusion.1
  230.7 77.0 %all-gather.2.cloned.1.call-done = bf16[512,2048]{1,0:T(8,128)(2,1)} async-done(((bf16[16,2048]{1,0:T(8,128)(2,1)}), bf16[512,2048]{1,0:T(8,128)(2,1)}) %all-gather.2.cloned.1.call-update) | async-done | bytes 2097168 | tf_op jit(solution)/shard_map/all_gather | solution.py:82
  307.7 3.1 fusion.55
  310.8 6.5 %collective-permute-start = (bf16[256,2048]{1,0:T(8,128)(2,1)}, bf16[256,2048]{1,0:T(8,128)(2,1)}, u32[]{:S(2)}, u32[]{:S(2)}) collective-permute-start(bf16[256,2048]{1,0:T(8,128)(2,1)} %get-tuple-element.34), channel_id=1, source_target_pairs={{0,32},{32,64},{64,96},{96,128},{128,160},{160,192},{192,224},{224... | collective-permute-start | bytes 3145736 | tf_op jit(solution)/shard_map/ppermute | solution.py:23
  317.5 12.0 %collective-permute-done = bf16[256,2048]{1,0:T(8,128)(2,1)} collective-permute-done((bf16[256,2048]{1,0:T(8,128)(2,1)}, bf16[256,2048]{1,0:T(8,128)(2,1)}, u32[]{:S(2)}, u32[]{:S(2)}) %collective-permute-start) | collective-permute-done | bytes 1048608 | tf_op jit(solution)/shard_map/ppermute | solution.py:23
  331.9 2.9 slice_bitcast_fusion.1
  334.8 2.4 fusion.57
  337.2 2.4 fusion.28
  339.6 2.1 multiply_reduce_fusion.1
  344.0 5.6 %all-to-all-start = ((bf16[32,16,2048]{2,1,0:T(8,128)(2,1)}), bf16[32,16,2048]{2,1,0:T(8,128)(2,1)}, u32[]{:S(2)}, u32[]{:S(2)}) async-start(bf16[32,16,2048]{2,1,0:T(8,128)(2,1)} %stack.2), calls=%async_computation.1 | async-start | bytes 4194304 | tf_op jit(solution)/shard_map/all_to_all | solution.py:11
  350.0 46.5 %all-to-all-done = bf16[32,16,2048]{2,1,0:T(8,128)(2,1)} async-done(((bf16[32,16,2048]{2,1,0:T(8,128)(2,1)}), bf16[32,16,2048]{2,1,0:T(8,128)(2,1)}, u32[]{:S(2)}, u32[]{:S(2)}) %all-to-all-start) | async-done | bytes 2097184 | tf_op jit(solution)/shard_map/all_to_all | solution.py:11
  396.5 3.3 collective-permute-start.3
  399.9 1.8 collective-permute-start.2
  402.0 6.5 %convolution_convert_fusion = bf16[512,3072]{1,0:T(8,128)(2,1)S(1)} fusion(bf16[512,1024]{1,0:T(8,128)(2,1)} %param.8, bf16[1024,3072]{1,0:T(8,128)(2,1)} %param.9), kind=kOutput, calls=%fused_computation.12 | convolution fusion | flops 3222798336 | bytes 10485760 | tf_op jit(solution)/shard_map/dot_general | solution.py:98
  408.5 1.8 slice_bitcast_fusion.2
  410.3 15.5 %collective-permute-done.3 = bf16[512,2048]{1,0:T(8,128)(2,1)S(1)} collective-permute-done((bf16[512,2048]{1,0:T(8,128)(2,1)}, bf16[512,2048]{1,0:T(8,128)(2,1)S(1)}, u32[]{:S(2)}, u32[]{:S(2)}) %collective-permute-start.3) | collective-permute-done | bytes 2097184 | tf_op jit(solution)/shard_map/ppermute | solution.py:25
  425.9 4.9 %pad_maximum_fusion = bf16[1536,2048]{1,0:T(8,128)(2,1)} fusion(bf16[512,2048]{1,0:T(8,128)(2,1)S(1)} %collective-permute-done.3, bf16[512,2048]{1,0:T(8,128)(2,1)} %bitcast.2, bf16[512,2048]{1,0:T(8,128)(2,1)S(1)} %collective-permute-done.2), kind=kLoop, calls=%fused_computation.7 | loop fusion | flops 18874368 | bytes 12582912 | tf_op jit(solution)/shard_map/concatenate | solution.py:21
  430.8 6.0 %gather_fusion = bf16[256,2048]{1,0:T(8,128)(2,1)S(1)} fusion(bf16[1536,2048]{1,0:T(8,128)(2,1)} %pad_maximum_fusion, s32[1024]{0:T(1024)S(1)} %pad_clamp_fusion), kind=kCustom, calls=%fused_computation | custom fusion | bytes 2098176 | tf_op jit(solution)/shard_map/while/body/eval_jaxpr/jit(_take)/gather | solution.py:121
  439.4 2.6 copy.22
  442.0 7.7 %fusion.13 = f32[8,512,768]{2,1,0:T(8,128)} fusion(bf16[64,8,8,128]{3,2,1,0:T(8,128)(2,1)S(1)} %copy-done.4, bf16[256,1024]{1,0:T(8,128)(2,1)} %get-tuple-element.36, bf16[512,1024]{1,0:T(8,128)(2,1)} %get-tuple-element.22), kind=kOutput, calls=%fused_computation.25 | convolution fusion | flops 808452096 | bytes 15204352 | tf_op jit(solution)/shard_map/while/body/eval_jaxpr/qhd,khd->hqk/dot_general | solution.py:38
  449.7 16.2 %fusion.58 = (f32[8,512]{1,0:T(8,128)S(1)}, f32[8,512,768]{2,1,0:T(8,128)}) fusion(f32[8,512,768]{2,1,0:T(8,128)} %fusion.13, pred[512,768]{1,0:T(8,128)(4,1)S(1)} %concatenate.20), kind=kOutput, calls=%fused_computation.102 | output fusion | flops 18875136 | bytes 25575424 | tf_op jit(solution)/shard_map/while/body/eval_jaxpr/sub | solution.py:42
  466.0 6.9 %fusion.16 = bf16[8,128,512]{2,1,0:T(8,128)(2,1)S(1)} fusion(bf16[768,8,128]{0,2,1:T(8,128)(2,1)S(1)} %bitcast.74, f32[8,512,768]{2,1,0:T(8,128)} %get-tuple-element.43, f32[8,512]{1,0:T(8,128)S(1)} %get-tuple-element.42), kind=kOutput, calls=%fused_computation.31 | convolution fusion | flops 812122112 | bytes 15220736 | tf_op jit(solution)/shard_map/while/body/eval_jaxpr/hqk,khd->qhd/dot_general | solution.py:44
  (52 shorter events, 12.1 us)
Async XLA Ops:
  6.5 466.3 %copy-start = (bf16[1024,1024]{1,0:T(8,128)(2,1)S(1)}, bf16[1024,1024]{1,0:T(8,128)(2,1)}, u32[]{:S(2)}) copy-start(bf16[1024,1024]{1,0:T(8,128)(2,1)} %param.12) | copy-start | bytes 6291460
  6.5 219.7 %reduce-scatter.2.cloned.1.call-start = ((), (), s32[]{:S(2)}) async-start(), calls=%async_computation.2 | async-start | bytes 1081344 | tf_op jit(solution)/shard_map/reduce_scatter | solution.py:67
  9.7 298.0 %all-gather.2.cloned.1.call-start = ((), (), s32[]{:S(2)}) async-start(), calls=%async_computation.3 | async-start | bytes 2162688 | tf_op jit(solution)/shard_map/all_gather | solution.py:82
  310.8 18.6 %collective-permute-start = (bf16[256,2048]{1,0:T(8,128)(2,1)}, bf16[256,2048]{1,0:T(8,128)(2,1)}, u32[]{:S(2)}, u32[]{:S(2)}) collective-permute-start(bf16[256,2048]{1,0:T(8,128)(2,1)} %get-tuple-element.34), channel_id=1, source_target_pairs={{0,32},{32,64},{64,96},{96,128},{128,160},{160,192},{192,224},{224... | collective-permute-start | bytes 3145736 | tf_op jit(solution)/shard_map/ppermute | solution.py:23
  317.4 14.4 %collective-permute-start.1 = (bf16[256,2048]{1,0:T(8,128)(2,1)}, bf16[256,2048]{1,0:T(8,128)(2,1)S(1)}, u32[]{:S(2)}, u32[]{:S(2)}) collective-permute-start(bf16[256,2048]{1,0:T(8,128)(2,1)} %get-tuple-element.32), channel_id=1, source_target_pairs={{32,0},{64,32},{96,64},{128,96},{160,128},{192,160},{224,192},{0,2... | collective-permute-start | bytes 3145736 | tf_op jit(solution)/shard_map/ppermute | solution.py:25
  317.4 13.4 %copy-start.1 = (bf16[512,2048]{1,0:T(8,128)(2,1)S(1)}, bf16[512,2048]{1,0:T(8,128)(2,1)}, u32[]{:S(2)}) copy-start(bf16[512,2048]{1,0:T(8,128)(2,1)} %all-gather.2.cloned.1.call-done) | copy-start | bytes 6291460
  337.2 4.5 copy-start.2
  342.4 7.2 %copy-start.6 = (s32[2,8]{1,0:T(2,128)S(1)}, s32[2,8]{1,0:T(2,128)}, u32[]{:S(2)}) copy-start(s32[2,8]{1,0:T(2,128)} %param.15) | copy-start | bytes 196
  344.0 52.5 %all-to-all-start = ((bf16[32,16,2048]{2,1,0:T(8,128)(2,1)}), bf16[32,16,2048]{2,1,0:T(8,128)(2,1)}, u32[]{:S(2)}, u32[]{:S(2)}) async-start(bf16[32,16,2048]{2,1,0:T(8,128)(2,1)} %stack.2), calls=%async_computation.1 | async-start | bytes 4194304 | tf_op jit(solution)/shard_map/all_to_all | solution.py:11
  396.5 29.3 %collective-permute-start.3 = (bf16[512,2048]{1,0:T(8,128)(2,1)}, bf16[512,2048]{1,0:T(8,128)(2,1)S(1)}, u32[]{:S(2)}, u32[]{:S(2)}) collective-permute-start(bf16[512,2048]{1,0:T(8,128)(2,1)} %bitcast.2), channel_id=1, source_target_pairs={{32,0},{64,32},{96,64},{128,96},{160,128},{192,160},{224,192},{0,2... | collective-permute-start | bytes 6291464 | tf_op jit(solution)/shard_map/ppermute | solution.py:25
  399.9 26.0 %collective-permute-start.2 = (bf16[512,2048]{1,0:T(8,128)(2,1)}, bf16[512,2048]{1,0:T(8,128)(2,1)S(1)}, u32[]{:S(2)}, u32[]{:S(2)}) collective-permute-start(bf16[512,2048]{1,0:T(8,128)(2,1)} %bitcast.2), channel_id=1, source_target_pairs={{0,32},{32,64},{64,96},{96,128},{128,160},{160,192},{192,224},{224... | collective-permute-start | bytes 6291464 | tf_op jit(solution)/shard_map/ppermute | solution.py:23
  436.8 1.3 copy-start.3
  438.1 3.9 copy-start.4
  449.7 16.2 %copy-start.5 = (bf16[768,1024]{0,1:T(8,128)(2,1)S(1)}, bf16[768,1024]{0,1:T(8,128)(2,1)}, u32[]{:S(2)}) copy-start(bf16[768,1024]{0,1:T(8,128)(2,1)} %copy.22) | copy-start | bytes 4718596
Sparse Core Ops, SparseCore 0:
  11.1 215.0 reduce-scatter.1
  230.8 76.8 all-gather.1
